TPU v7x, 256 devices: a whole 4x4x8 slice. The times are simulated.
256 devices in a mesh: row: 16 (over z_hi, y, core), col: 16 (over z_lo, x).
Axes of the slice: x: 4, y: 4, z: 8 (z_hi: 2, z_lo: 4; z = z_hi * 4 + z_lo), core: 2. Of those that a mesh axis runs over, the one named last changes fastest.
Arguments:
- tokens: bfloat16 [2048, 8192], P('col', 'row'), may hold values from -6 to 6
- gate_vals: bfloat16 [448, 64, 4096], P('col', 'row'), may hold values from -0.09375 to 0.09375
- gate_scales: float32 [448, 64], P('col', 'row'), may hold values from 0.3 to 3
- gate_rows: int32 [448, 64], P('col', 'row'), may hold values from 0 to 127, as said below
- up_vals: bfloat16 [448, 64, 4096], P('col', 'row'), may hold values from -0.09375 to 0.09375
- up_scales: float32 [448, 64], P('col', 'row'), may hold values from 0.3 to 3
- up_rows: int32 [448, 64], P('col', 'row'), may hold values from 0 to 127, as said below
- down_vals: bfloat16 [128, 224, 4096], P('row', 'col'), may hold values from -0.046875 to 0.046875
- down_scales: float32 [128, 224], P('row', 'col'), may hold values from 0.3 to 3
- down_rows: int32 [128, 224], P('row', 'col'), may hold values from 0 to 447, as said below
Outputs:
- mixed: bfloat16 [2048, 8192], P('col', 'row')
Inputs may be any that keep to these rules, and one draw needn't show every extreme that they name: Row j of gate_rows holds distinct block rows; slots k with the same k // 4 hold exactly half of the block rows from (k // 4) * 8 to that plus 8 - 1, in increasing order. `up_rows`: same law as gate_rows, drawn independently. Row j of down_rows holds distinct block rows of the hidden units; slots k with the same k // 14 hold exactly half of the block rows from (k // 14) * 28 to that plus 28 - 1, in increasing order.
All inputs are finite; a program needn't handle non-finite values.
Results may differ from a plain program's by a relative error of at most 0.03.
Values may be sent and summed in bfloat16 or wider, within the bound.
A program may use at most 128 MiB of HBM per device.

v0:
```python
import jax
import jax.numpy as jnp
from jax import lax
from jax.sharding import PartitionSpec as P

BLOCK = 64


def dense_panel(values, scales, indices, offset, groups):
    blocks = (values.astype(jnp.float32) * scales[:, :, None]).astype(jnp.bfloat16)
    onehot = (
        indices[:, :, None] - offset == jnp.arange(groups, dtype=jnp.int32)[None, None, :]
    ).astype(jnp.bfloat16)
    matrix = jnp.einsum("jkg,jkc->gjc", onehot, blocks, preferred_element_type=jnp.float32).astype(
        jnp.bfloat16
    )
    matrix = matrix.reshape(groups, values.shape[0], BLOCK, BLOCK).transpose(0, 2, 1, 3)
    return matrix.reshape(groups * BLOCK, values.shape[0] * BLOCK)


def swish_gate(summed, ff_local):
    return (jax.nn.silu(summed[:, :ff_local]) * summed[:, ff_local:]).astype(jnp.bfloat16)


def per_device(
    tokens,
    gate_vals,
    gate_scales,
    gate_rows,
    up_vals,
    up_scales,
    up_rows,
    down_vals,
    down_scales,
    down_rows,
):
    group_size = tokens.shape[1] // BLOCK
    row_offset = lax.axis_index("row") * group_size
    w_gate = dense_panel(gate_vals, gate_scales, gate_rows, row_offset, group_size)
    w_up = dense_panel(up_vals, up_scales, up_rows, row_offset, group_size)
    joined = jnp.concatenate([w_gate, w_up], axis=1)
    ff_local = w_gate.shape[1]
    ff_groups = ff_local // BLOCK
    w_down = dense_panel(
        down_vals, down_scales, down_rows, lax.axis_index("col") * ff_groups, ff_groups
    )
    gathered = lax.all_gather(tokens, "col", axis=0, tiled=True)
    selected = gathered
    summed = lax.psum_scatter(
        jnp.dot(selected, joined, preferred_element_type=jnp.float32).astype(jnp.bfloat16),
        "row",
        scatter_dimension=0,
        tiled=True,
    ).astype(jnp.float32)
    hidden_part = swish_gate(summed, ff_local)
    hidden = lax.all_gather(hidden_part, "row", axis=0, tiled=True)
    selected = hidden
    return lax.psum_scatter(
        jnp.dot(selected, w_down, preferred_element_type=jnp.float32).astype(jnp.bfloat16),
        "col",
        scatter_dimension=0,
        tiled=True,
    )


def solution(mesh):
    placed = (
        P("col", "row"),
        P("col", "row", None),
        P("col", "row"),
        P("col", "row"),
        P("col", "row", None),
        P("col", "row"),
        P("col", "row"),
        P("row", "col", None),
        P("row", "col"),
        P("row", "col"),
    )
    return jax.shard_map(
        per_device, mesh=mesh, in_specs=placed, out_specs=P("col", "row"), check_vma=False
    )
```

profile of v0, /device:TPU:8, one launch (start us, length us, event | category | flops | bytes accessed | tf_op | source)
XLA Modules:
  0.0 520.2 jit_solution(7833358821904089959)
XLA Ops:
  6.5 0.7 all-gather.3.cloned.1.call-update
  8.1 0.8 copy.27
  8.9 2.4 fusion.2
  11.3 4.9 reshape.27
  16.2 6.2 %copy.29 = bf16[8,28,64,64]{2,0,3,1:T(8,128)(2,1)} copy(bf16[8,28,64,64]{3,2,0,1:T(8,128)(2,1)} %reshape.27) | data formatting | bytes 3670016 | tf_op jit(solution)/shard_map/reshape | solution.py:17
  22.4 5.1 reshape.28
  27.7 2.5 fusion.3
  30.2 6.3 %reshape.29 = bf16[8,28,64,64]{3,2,0,1:T(8,128)(2,1)} reshape(bf16[8,28,4096]{2,0,1:T(8,128)(2,1)} %fusion.3) | data formatting | bytes 3670016 | tf_op jit(solution)/shard_map/reshape | solution.py:17
  36.6 6.2 %copy.32 = bf16[8,28,64,64]{2,0,3,1:T(8,128)(2,1)} copy(bf16[8,28,64,64]{3,2,0,1:T(8,128)(2,1)} %reshape.29) | data formatting | bytes 3670016 | tf_op jit(solution)/shard_map/reshape | solution.py:17
  42.8 5.9 %reshape.30 = bf16[512,1792]{0,1:T(8,128)(2,1)} reshape(bf16[8,64,28,64]{1,0,3,2:T(8,128)(2,1)} %bitcast.30) | data formatting | bytes 3670016 | tf_op jit(solution)/shard_map/reshape | solution.py:18
  48.7 46.1 %all-gather.3.cloned.1.call-done = bf16[2048,512]{1,0:T(8,128)(2,1)} async-done(((bf16[128,512]{1,0:T(8,128)(2,1)}), bf16[2048,512]{1,0:T(8,128)(2,1)}) %all-gather.3.cloned.1.call-update) | async-done | bytes 2097168 | tf_op jit(solution)/shard_map/all_gather | solution.py:47
  94.8 12.9 %fusion = bf16[2048,3584]{0,1:T(8,128)(2,1)} fusion(bf16[2048,512]{1,0:T(8,128)(2,1)} %all-gather.3.cloned.1.call-done, bf16[512,1792]{0,1:T(8,128)(2,1)} %reshape.30, bf16[512,1792]{0,1:T(8,128)(2,1)S(1)} %reshape.28), kind=kOutput, calls=%fused_computation.1 | convolution fusion | flops 7530872832 | bytes 20447232 | tf_op jit(solution)/shard_map/dot_general | solution.py:50
  107.6 18.7 %copy.37 = bf16[2048,3584]{1,0:T(8,128)(2,1)} copy(bf16[2048,3584]{0,1:T(8,128)(2,1)} %fusion) | data formatting | bytes 29360128
  126.4 191.3 %reduce-scatter.7.cloned.1.call-done = bf16[128,3584]{1,0:T(8,128)(2,1)} async-done(((bf16[2048,3584]{1,0:T(8,128)(2,1)}), bf16[128,3584]{1,0:T(8,128)(2,1)}) %reduce-scatter.7.cloned.1.call-update) | async-done | bytes 917520
  317.8 1.5 copy.38
  319.5 1.0 fusion.8
  321.1 1.3 fusion.1
  322.5 1.0 copy.35
  323.5 5.0 reshape.31
  328.4 7.5 %copy.36 = bf16[28,64,8,64]{3,2,1,0:T(8,128)(2,1)} copy(bf16[28,64,8,64]{3,1,2,0:T(8,128)(2,1)} %bitcast.31) | data formatting | bytes 3670016 | tf_op jit(solution)/shard_map/transpose | solution.py:17
  336.0 5.0 reshape.32
  341.0 79.6 %all-gather.5.cloned.1.call-done = bf16[2048,1792]{0,1:T(8,128)(2,1)} async-done(((bf16[128,1792]{0,1:T(8,128)(2,1)}), bf16[2048,1792]{0,1:T(8,128)(2,1)}) %all-gather.5.cloned.1.call-update) | async-done | bytes 7340048 | tf_op jit(solution)/shard_map/all_gather | solution.py:56
  420.6 8.5 %convolution_convert_fusion.4 = bf16[2048,512]{1,0:T(8,128)(2,1)} fusion(bf16[2048,1792]{0,1:T(8,128)(2,1)} %all-gather.5.cloned.1.call-done, bf16[1792,512]{1,0:T(8,128)(2,1)S(1)} %reshape.32), kind=kOutput, calls=%fused_computation.11 | convolution fusion | flops 3759144960 | bytes 11272192 | tf_op jit(solution)/shard_map/dot_general | solution.py:59
  429.1 84.5 %reduce-scatter.5.cloned.1.call-done = bf16[128,512]{1,0:T(8,128)(2,1)} async-done(((bf16[2048,512]{1,0:T(8,128)(2,1)}), bf16[128,512]{1,0:T(8,128)(2,1)}) %reduce-scatter.5.cloned.1.call-update) | async-done | bytes 131088 | tf_op jit(solution)/shard_map/reduce_scatter | solution.py:58
  (25 shorter events, 1.8 us)
Async XLA Ops:
  6.5 88.2 %all-gather.3.cloned.1.call-start = ((), (), s32[]{:S(2)}) async-start(), calls=%async_computation.2 | async-start | bytes 2228224 | tf_op jit(solution)/shard_map/all_gather | solution.py:47
  7.3 310.5 %reduce-scatter.7.cloned.1.call-start = ((), (), s32[]{:S(2)}) async-start(), calls=%async_computation.5 | async-start | bytes 15597568
  22.4 5.2 %copy-start.3 = (f32[28,4]{0,1:T(4,128)S(1)}, f32[28,4]{0,1:T(4,128)}, u32[]{:S(2)}) copy-start(f32[28,4]{0,1:T(4,128)} %param.15) | copy-start | bytes 1348
  22.4 5.3 %copy-start.4 = (bf16[28,4,4096]{2,1,0:T(4,128)(2,1)S(1)}, bf16[28,4,4096]{2,1,0:T(4,128)(2,1)}, u32[]{:S(2)}) copy-start(bf16[28,4,4096]{2,1,0:T(4,128)(2,1)} %param.14) | copy-start | bytes 2752516
  126.4 294.2 %all-gather.5.cloned.1.call-start = ((), (), s32[]{:S(2)}) async-start(), calls=%async_computation.3 | async-start | bytes 7798784 | tf_op jit(solution)/shard_map/all_gather | solution.py:56
  319.3 1.5 copy-start.1
  319.4 1.5 copy-start.2
  319.4 1.5 copy-start
  320.6 193.1 %reduce-scatter.5.cloned.1.call-start = ((), (), s32[]{:S(2)}) async-start(), calls=%async_computation.4 | async-start | bytes 2228224 | tf_op jit(solution)/shard_map/reduce_scatter | solution.py:58
Sparse Core Ops, SparseCore 0:
  9.1 85.6 all-gather.2
  126.5 191.2 reduce-scatter.6
  320.7 99.8 all-gather.4
  429.3 84.3 reduce-scatter.4
where the time goes:
time: 522 us; the launch traced here: 520 us
  waiting for transfers between devices  402 us (77%)
  local copies, waits for them, and re-layouts  74.7 us (14%)
  matrix products  27.6 us (5%)
  between operations  13.2 us (3%)
    unnamed x5, waiting for transfers between devices  192 us
    reduce_scatter x1, waiting for transfers between devices, per_device(): lax.psum_scatter(jnp.dot(selected, w_down, preferred_element_type=jnp.flo...  84.5 us
    all_gather x1, waiting for transfers between devices, per_device(): hidden = lax.all_gather(hidden_part, 'row', axis=0, tiled=True)  79.6 us
    all_gather x1, waiting for transfers between devices, per_device(): gathered = lax.all_gather(tokens, 'col', axis=0, tiled=True)  46.1 us
    reshape x5, local copies, waits for them, and re-layouts, dense_panel(): matrix.reshape(groups, values.shape[0], BLOCK, BLOCK).transpose(0, 2, 1, 3)  28.6 us
    unnamed x15, local copies, waits for them, and re-layouts  21.3 us
    reshape x3, local copies, waits for them, and re-layouts, dense_panel(): return matrix.reshape(groups * BLOCK, values.shape[0] * BLOCK)  16 us
    dot_general x1, matrix products, per_device(): jnp.dot(selected, joined, preferred_element_type=jnp.float32)  12.9 us
  transfers between devices with their start and end apart: 4, of which 4 were waited for; matrix products, arithmetic and copies ran while one was open for 12% of the time, Pallas kernels for 0%

commit v1 on v0

--- a/solution.py
+++ b/solution.py
@@ -44,7 +44,9 @@
     w_down = dense_panel(
         down_vals, down_scales, down_rows, lax.axis_index("col") * ff_groups, ff_groups
     )
-    gathered = lax.all_gather(tokens, "col", axis=0, tiled=True)
+    gathered = jnp.concatenate(
+        lax.all_to_all(jnp.stack([tokens] * lax.axis_size("col")), "col", 0, 0), axis=0
+    )
     selected = gathered
     summed = lax.psum_scatter(
         jnp.dot(selected, joined, preferred_element_type=jnp.float32).astype(jnp.bfloat16),

time: 522 us -> 495 us (0.948)
  waiting for transfers between devices: 402 us -> 363 us
  starting transfers between devices: 0.31 us -> 8.91 us
    all_gather x1 -> x0, waiting for transfers between devices: 46.1 us -> none  [per_device(): gathered = lax.all_gather(tokens, 'col', axis=0, tiled=True)]
    all_to_all x0 -> x1, starting transfers between devices: none -> 8.61 us  [per_device(): lax.all_to_all(jnp.stack([tokens] * lax.axis_size('col')), 'col', 0, 0)]
    unnamed x5 -> x4, waiting for transfers between devices: 192 us -> 198 us
    unnamed x15 -> x23, local copies, waits for them, and re-layouts: 21.3 us -> 20.7 us
  transfers between devices with their start and end apart: 4 -> 4, of which waited for: 4 -> 4; matrix products, arithmetic and copies ran while one was open for 12% -> 13% of each run, Pallas kernels for 0% -> 0%
where the time goes in v1:
time: 495 us; the launch traced here: 493 us
  waiting for transfers between devices  363 us (73%)
  local copies, waits for them, and re-layouts  78.8 us (16%)
  matrix products  27.9 us (6%)
  between operations  13.2 us (3%)
  starting transfers between devices  8.91 us (2%)
    unnamed x4, waiting for transfers between devices  198 us
    reduce_scatter x1, waiting for transfers between devices, per_device(): lax.psum_scatter(jnp.dot(selected, w_down, preferred_element_type=jnp.flo...  84.5 us
    all_gather x1, waiting for transfers between devices, per_device(): hidden = lax.all_gather(hidden_part, 'row', axis=0, tiled=True)  79.6 us
    reshape x5, local copies, waits for them, and re-layouts, dense_panel(): matrix.reshape(groups, values.shape[0], BLOCK, BLOCK).transpose(0, 2, 1, 3)  29.9 us
    unnamed x23, local copies, waits for them, and re-layouts  20.7 us
    reshape x3, local copies, waits for them, and re-layouts, dense_panel(): return matrix.reshape(groups * BLOCK, values.shape[0] * BLOCK)  16.9 us
    dot_general x1, matrix products, per_device(): jnp.dot(selected, joined, preferred_element_type=jnp.float32)  13.1 us
  transfers between devices with their start and end apart: 4, of which 4 were waited for; matrix products, arithmetic and copies ran while one was open for 13% of the time, Pallas kernels for 0%

profile of v1, /device:TPU:8, one launch (start us, length us, event | category | flops | bytes accessed | tf_op | source)
XLA Modules:
  0.0 493.1 jit_solution(4012081200027790918)
XLA Ops:
  6.5 2.5 stack.2
  9.1 8.6 %all-to-all-start = ((bf16[16,128,512]{2,1,0:T(8,128)(2,1)}), bf16[16,128,512]{2,1,0:T(8,128)(2,1)S(1)}, u32[]{:S(2)}, u32[]{:S(2)}) async-start(bf16[16,128,512]{2,1,0:T(8,128)(2,1)} %stack.2), calls=%async_computation | async-start | bytes 4194304 | tf_op jit(solution)/shard_map/all_to_all | solution.py:48
  18.0 2.5 fusion.2
  20.4 6.3 %reshape.32 = bf16[8,28,64,64]{3,2,0,1:T(8,128)(2,1)} reshape(bf16[8,28,4096]{2,0,1:T(8,128)(2,1)} %fusion.2) | data formatting | bytes 3670016 | tf_op jit(solution)/shard_map/reshape | solution.py:17
  26.8 6.2 %copy.29 = bf16[8,28,64,64]{2,0,3,1:T(8,128)(2,1)} copy(bf16[8,28,64,64]{3,2,0,1:T(8,128)(2,1)} %reshape.32) | data formatting | bytes 3670016 | tf_op jit(solution)/shard_map/reshape | solution.py:17
  33.0 6.0 %reshape.33 = bf16[512,1792]{0,1:T(8,128)(2,1)} reshape(bf16[8,64,28,64]{1,0,3,2:T(8,128)(2,1)} %bitcast.30) | data formatting | bytes 3670016 | tf_op jit(solution)/shard_map/reshape | solution.py:18
  39.2 2.5 fusion.3
  41.6 6.3 %reshape.34 = bf16[8,28,64,64]{3,2,0,1:T(8,128)(2,1)} reshape(bf16[8,28,4096]{2,0,1:T(8,128)(2,1)} %fusion.3) | data formatting | bytes 3670016 | tf_op jit(solution)/shard_map/reshape | solution.py:17
  47.9 6.2 %copy.32 = bf16[8,28,64,64]{2,0,3,1:T(8,128)(2,1)} copy(bf16[8,28,64,64]{3,2,0,1:T(8,128)(2,1)} %reshape.34) | data formatting | bytes 3670016 | tf_op jit(solution)/shard_map/reshape | solution.py:17
  54.1 5.9 %reshape.35 = bf16[512,1792]{0,1:T(8,128)(2,1)} reshape(bf16[8,64,28,64]{1,0,3,2:T(8,128)(2,1)} %bitcast.31) | data formatting | bytes 3670016 | tf_op jit(solution)/shard_map/reshape | solution.py:18
  60.0 0.6 all-to-all-done
  60.6 13.1 %fusion = bf16[2048,3584]{0,1:T(8,128)(2,1)} fusion(bf16[2048,512]{1,0:T(8,128)(2,1)S(1)} %bitcast.33, bf16[512,1792]{0,1:T(8,128)(2,1)} %reshape.35, bf16[512,1792]{0,1:T(8,128)(2,1)} %reshape.33), kind=kOutput, calls=%fused_computation.1 | convolution fusion | flops 7530872832 | bytes 20447232 | tf_op jit(solution)/shard_map/dot_general | solution.py:52
  73.7 18.8 %copy.37 = bf16[2048,3584]{1,0:T(8,128)(2,1)} copy(bf16[2048,3584]{0,1:T(8,128)(2,1)} %fusion) | data formatting | bytes 29360128
  92.6 198.2 %reduce-scatter.7.cloned.1.call-done = bf16[128,3584]{1,0:T(8,128)(2,1)} async-done(((bf16[2048,3584]{1,0:T(8,128)(2,1)}), bf16[128,3584]{1,0:T(8,128)(2,1)}) %reduce-scatter.7.cloned.1.call-update) | async-done | bytes 917520
  290.8 1.5 copy.38
  292.5 1.0 fusion.8
  294.1 1.3 fusion.1
  295.4 1.0 copy.35
  296.4 4.9 %reshape.37 = bf16[28,8,64,64]{3,2,1,0:T(8,128)(2,1)} reshape(bf16[28,8,4096]{2,1,0:T(8,128)(2,1)S(1)} %copy.35) | data formatting | bytes 3670016 | tf_op jit(solution)/shard_map/reshape | solution.py:17
  301.4 7.5 %copy.36 = bf16[28,64,8,64]{3,2,1,0:T(8,128)(2,1)} copy(bf16[28,64,8,64]{3,1,2,0:T(8,128)(2,1)} %bitcast.32) | data formatting | bytes 3670016 | tf_op jit(solution)/shard_map/transpose | solution.py:17
  308.9 5.0 %reshape.38 = bf16[1792,512]{1,0:T(8,128)(2,1)S(1)} reshape(bf16[28,64,8,64]{3,2,1,0:T(8,128)(2,1)} %copy.36) | data formatting | bytes 3670016 | tf_op jit(solution)/shard_map/reshape | solution.py:18
  313.9 79.6 %all-gather.2.cloned.1.call-done = bf16[2048,1792]{0,1:T(8,128)(2,1)} async-done(((bf16[128,1792]{0,1:T(8,128)(2,1)}), bf16[2048,1792]{0,1:T(8,128)(2,1)}) %all-gather.2.cloned.1.call-update) | async-done | bytes 7340048 | tf_op jit(solution)/shard_map/all_gather | solution.py:58
  393.5 8.6 %convolution_convert_fusion.4 = bf16[2048,512]{1,0:T(8,128)(2,1)} fusion(bf16[2048,1792]{0,1:T(8,128)(2,1)} %all-gather.2.cloned.1.call-done, bf16[1792,512]{1,0:T(8,128)(2,1)S(1)} %reshape.38), kind=kOutput, calls=%fused_computation.11 | convolution fusion | flops 3759144960 | bytes 11272192 | tf_op jit(solution)/shard_map/dot_general | solution.py:61
  402.1 84.5 %reduce-scatter.5.cloned.1.call-done = bf16[128,512]{1,0:T(8,128)(2,1)} async-done(((bf16[2048,512]{1,0:T(8,128)(2,1)}), bf16[128,512]{1,0:T(8,128)(2,1)}) %reduce-scatter.5.cloned.1.call-update) | async-done | bytes 131088 | tf_op jit(solution)/shard_map/reduce_scatter | solution.py:60
  (33 shorter events, 1.2 us)
Async XLA Ops:
  9.0 8.7 %copy-start.3 = (s32[28,4]{0,1:T(4,128)S(1)}, s32[28,4]{0,1:T(4,128)}, u32[]{:S(2)}) copy-start(s32[28,4]{0,1:T(4,128)} %param.16) | copy-start | bytes 1348
  9.0 8.7 %copy-start.4 = (s32[28,4]{0,1:T(4,128)S(1)}, s32[28,4]{0,1:T(4,128)}, u32[]{:S(2)}) copy-start(s32[28,4]{0,1:T(4,128)} %param.13) | copy-start | bytes 1348
  9.0 8.8 %copy-start.5 = (f32[28,4]{0,1:T(4,128)S(1)}, f32[28,4]{0,1:T(4,128)}, u32[]{:S(2)}) copy-start(f32[28,4]{0,1:T(4,128)} %param.12) | copy-start | bytes 1348
  9.0 8.9 %copy-start.7 = (bf16[28,4,4096]{2,1,0:T(4,128)(2,1)S(1)}, bf16[28,4,4096]{2,1,0:T(4,128)(2,1)}, u32[]{:S(2)}) copy-start(bf16[28,4,4096]{2,1,0:T(4,128)(2,1)} %param.11) | copy-start | bytes 2752516
  9.1 51.6 %all-to-all-start = ((bf16[16,128,512]{2,1,0:T(8,128)(2,1)}), bf16[16,128,512]{2,1,0:T(8,128)(2,1)S(1)}, u32[]{:S(2)}, u32[]{:S(2)}) async-start(bf16[16,128,512]{2,1,0:T(8,128)(2,1)} %stack.2), calls=%async_computation | async-start | bytes 4194304 | tf_op jit(solution)/shard_map/all_to_all | solution.py:48
  17.7 273.1 %reduce-scatter.7.cloned.1.call-start = ((), (), s32[]{:S(2)}) async-start(), calls=%async_computation.5 | async-start | bytes 15597568
  32.9 6.1 %copy-start.6 = (f32[28,4]{0,1:T(4,128)S(1)}, f32[28,4]{0,1:T(4,128)}, u32[]{:S(2)}) copy-start(f32[28,4]{0,1:T(4,128)} %param.15) | copy-start | bytes 1348
  32.9 6.2 %copy-start.8 = (bf16[28,4,4096]{2,1,0:T(4,128)(2,1)S(1)}, bf16[28,4,4096]{2,1,0:T(4,128)(2,1)}, u32[]{:S(2)}) copy-start(bf16[28,4,4096]{2,1,0:T(4,128)(2,1)} %param.14) | copy-start | bytes 2752516
  92.5 301.0 %all-gather.2.cloned.1.call-start = ((), (), s32[]{:S(2)}) async-start(), calls=%async_computation.3 | async-start | bytes 7798784 | tf_op jit(solution)/shard_map/all_gather | solution.py:58
  292.3 1.4 copy-start.1
  292.3 1.5 copy-start.2
  292.3 1.5 copy-start
  293.5 193.1 %reduce-scatter.5.cloned.1.call-start = ((), (), s32[]{:S(2)}) async-start(), calls=%async_computation.4 | async-start | bytes 2228224 | tf_op jit(solution)/shard_map/reduce_scatter | solution.py:60
Sparse Core Ops, SparseCore 0:
  92.7 198.0 reduce-scatter.6
  293.6 99.8 all-gather.1
  402.2 84.3 reduce-scatter.4
